TPU v7x, 32 devices: a whole 2x2x4 slice. The times are simulated.
32 devices in a mesh: group: 2 (over y), expert: 4 (over z), etp: 4 (over x, core).
Axes of the slice: x: 2, y: 2, z: 4, core: 2. Of those that a mesh axis runs over, the one named last changes fastest.
Arguments:
- tokens: bfloat16 [128, 4096], P(('group', 'expert')), parts along dimension 0, may hold values from -6 to 6
- expert_ids: int32 [128, 2], P(('group', 'expert')), parts along dimension 0, may hold values from 0 to 3, all different within a row; in each aligned block of 4 rows (0 to 3, 4 to 7, ...) at most 4 rows name the same one
- route_weights: float32 [128, 2], P(('group', 'expert', 'etp')), parts along dimension 0, may hold values from 0.05 to 1
- w_gate: bfloat16 [4, 1536, 4096], P('expert', 'etp'), may hold values from -0.09375 to 0.09375
- w_up: bfloat16 [4, 1536, 4096], P('expert', 'etp'), may hold values from -0.09375 to 0.09375
- w_down: bfloat16 [4, 1536, 4096], P('expert', 'etp'), may hold values from -0.15625 to 0.15625
Outputs:
- mixed: bfloat16 [128, 4096], P(('group', 'expert', 'etp')), parts along dimension 0
There are 2 independent parts, one for each index of `group`. A program takes and returns all parts, laid end to end along the dimension named above; an argument that names none is the same for every part. Nothing has to cross between parts.
Inputs may be any that keep to these rules, and one draw needn't show every extreme that they name: `expert_ids`: each row names 2 different experts; in each aligned block of 4 rows no expert is named by more than 4 rows, a bound that some block reaches.
All inputs are finite; a program needn't handle non-finite values.
Results may differ from a plain program's by a relative error of at most 0.015.
Values may be sent and summed in bfloat16 or wider, within the bound.
A program may use at most 64 MiB of HBM per device.

v0:
```python
import jax
import jax.numpy as jnp
from jax import lax
from jax.sharding import PartitionSpec as P


def slot_layout(expert_ids, experts, rows_dev, n_blocks):
    flat = expert_ids.reshape(-1)
    count = flat.shape[0]
    top = expert_ids.shape[1]
    row = jnp.arange(count, dtype=jnp.int32) // top
    block = row // rows_dev
    by_block = expert_ids.reshape(n_blocks, rows_dev * top)
    onehot = (by_block[:, :, None] == jnp.arange(experts, dtype=jnp.int32)[None, None, :]).astype(
        jnp.int32
    )
    ranks = jnp.cumsum(onehot, axis=1) - onehot
    slot = jnp.sum(ranks * onehot, axis=2).reshape(-1)
    return (flat, block, slot)


def on_device(tokens, expert_ids, route_weights, w_gate, w_up, w_down):
    n_expert = lax.axis_size("expert")
    n_etp = lax.axis_size("etp")
    exp_dev = w_gate.shape[0]
    width = tokens.shape[1]
    experts = n_expert * exp_dev
    tok_dev, top = expert_ids.shape
    rows_dev = tok_dev // n_etp
    capsub = max(2, 2 * rows_dev * top // experts)
    flat, block, slot = slot_layout(expert_ids, experts, rows_dev, n_etp)
    dest = (flat * n_etp + block) * capsub + slot
    repeated = jnp.repeat(tokens, top, axis=0)
    send = jnp.zeros((experts * n_etp * capsub, width), jnp.bfloat16).at[dest].set(repeated)
    send = send.reshape(n_expert, exp_dev, n_etp, capsub, width)
    received = lax.all_to_all(send, "expert", split_axis=0, concat_axis=0, tiled=True)
    gate = jnp.einsum("sepcd,efd->sepcf", received, w_gate, preferred_element_type=jnp.float32)
    upper = jnp.einsum("sepcd,efd->sepcf", received, w_up, preferred_element_type=jnp.float32)
    hidden = (jax.nn.silu(gate) * upper).astype(jnp.bfloat16)
    partial_out = jnp.einsum("sepcf,efd->sepcd", hidden, w_down, preferred_element_type=jnp.float32)
    summed = lax.psum_scatter(
        partial_out.astype(jnp.bfloat16), "etp", scatter_dimension=2, tiled=True
    )
    back = lax.all_to_all(summed, "expert", split_axis=0, concat_axis=0, tiled=True)
    results = back.reshape(experts * capsub, width)
    own_count = rows_dev * top
    own_start = lax.axis_index("etp") * own_count
    own_expert = lax.dynamic_slice_in_dim(flat, own_start, own_count, 0)
    own_slot = lax.dynamic_slice_in_dim(slot, own_start, own_count, 0)
    index = own_expert * capsub + own_slot
    picked = results[index].astype(jnp.float32).reshape(rows_dev, top, width)
    combine = route_weights / jnp.sum(route_weights, axis=1, keepdims=True)
    return jnp.sum(picked * combine[:, :, None], axis=1).astype(jnp.bfloat16)


def solution(mesh):
    in_specs = (
        P(("group", "expert"), None),
        P(("group", "expert"), None),
        P(("group", "expert", "etp"), None),
        P("expert", "etp", None),
        P("expert", "etp", None),
        P("expert", "etp", None),
    )
    out_specs = P(("group", "expert", "etp"), None)
    return jax.shard_map(
        on_device, mesh=mesh, in_specs=in_specs, out_specs=out_specs, check_vma=False
    )
```

profile of v0, /device:TPU:0, one launch (start us, length us, event | category | flops | bytes accessed | tf_op | source)
XLA Modules:
  0.0 96.3 jit_solution(16440530250967646768)
XLA Ops:
  6.5 0.0 copy-start
  6.5 0.0 all-reduce.3.cloned.1.call-start
  6.5 0.8 broadcast_multiply_fusion
  7.4 0.9 copy.21
  8.3 0.1 copy.20
  8.3 0.1 mul.48
  8.4 0.1 eq.15
  8.5 0.7 reduce_window_sum.11
  9.3 0.1 reshape.160
  9.3 1.1 %broadcast_in_dim.14 = bf16[16,2,4096]{2,1,0:T(2,128)(2,1)S(1)} broadcast(bf16[16,4096]{1,0:T(8,128)(2,1)} %param.6), dimensions={0,2} | broadcast | bytes 393216 | tf_op jit(solution)/shard_map/broadcast_in_dim | solution.py:33
  10.4 0.8 reshape.184
  11.3 2.2 %scatter_custom_fusion = bf16[64,4096]{1,0:T(8,128)(2,1)} fusion(s32[32]{0:T(128)S(1)} %fusion.26, bf16[32,4096]{1,0:T(8,128)(2,1)} %reshape.184, bf16[]{:T(256)} %constant.42.clone.1), kind=kCustom, calls=%fused_computation.16 | custom fusion | bytes 524800 | tf_op jit(solution)/shard_map/scatter | solution.py:34
  13.5 2.0 %reshape.162 = bf16[4,1,4,4,4096]{4,3,2,1,0:T(4,128)(2,1)} reshape(bf16[64,4096]{1,0:T(8,128)(2,1)} %scatter_custom_fusion) | data formatting | bytes 1048576 | tf_op jit(solution)/shard_map/reshape | solution.py:35
  15.5 20.8 %all_to_all.10 = bf16[4,1,4,4,4096]{4,3,2,1,0:T(4,128)(2,1)S(1)} all-to-all(bf16[4,1,4,4,4096]{4,3,2,1,0:T(4,128)(2,1)} %reshape.162), channel_id=1, replica_groups=mesh['group'=2,'expert'=4,'etp'=4] {'expert'}, dimensions={0} | all-to-all | bytes 1048576 | tf_op jit(solution)/shard_map/all_to_all | solution.py:36
  36.4 0.0 copy-start.2
  36.4 3.2 %fusion.6 = f32[4,1,4,4,384]{4,3,2,0,1:T(4,128)S(1)} fusion(bf16[1,384,4096]{2,1,0:T(8,128)(2,1)} %param.9, bf16[4,1,4,4,4096]{4,3,2,1,0:T(4,128)(2,1)S(1)} %all_to_all.10), kind=kOutput, calls=%fused_computation.9 | convolution fusion | flops 201326592 | bytes 3768320 | tf_op jit(solution)/shard_map/sepcd,efd->sepcf/dot_general | solution.py:37
  39.6 0.0 copy-done.2
  39.6 1.2 %fusion.18 = bf16[4,4,4,384]{3,2,1,0:T(4,128)(2,1)S(1)} fusion(bf16[1,384,4096]{2,1,0:T(8,128)(2,1)S(1)} %copy-done.2, bf16[4,1,4,4,4096]{4,3,2,1,0:T(4,128)(2,1)S(1)} %all_to_all.10, f32[4,1,4,4,384]{4,3,2,0,1:T(4,128)S(1)} %fusion.6), kind=kOutput, calls=%fused_computation.13 | convolution fusion | flops 201474048 | bytes 3817472 | tf_op jit(solution)/shard_map/sepcd,efd->sepcf/dot_general | solution.py:38
  40.9 0.0 copy-done
  40.9 0.0 copy-start.1
  40.9 0.0 copy-start.3
  40.9 1.5 %fusion = bf16[4,1,4,4,4096]{4,3,2,0,1:T(4,128)(2,1)} fusion(bf16[4,4,4,384]{3,2,1,0:T(4,128)(2,1)S(1)} %fusion.18, bf16[1,384,4096]{2,1,0:T(8,128)(2,1)S(1)} %copy-done), kind=kOutput, calls=%fused_computation.3 | convolution fusion | flops 201588736 | bytes 3719168 | tf_op jit(solution)/shard_map/sepcf,efd->sepcd/dot_general | solution.py:40
  42.4 0.0 all-reduce.3.cloned.1.call-update
  42.4 0.1 reshape.169
  42.5 0.1 reshape.170
  42.6 0.0 copy-done.1
  42.6 0.1 copy.24
  42.7 0.0 copy-done.3
  42.7 0.6 dynamic-slice
  43.3 31.8 %all-reduce.3.cloned.1.call-done = bf16[4,1,4,4,4096]{4,3,2,0,1:T(4,128)(2,1)} async-done(((bf16[4,1,4,4,4096]{4,3,2,0,1:T(4,128)(2,1)}), bf16[4,1,4,4,4096]{4,3,2,0,1:T(4,128)(2,1)}) %all-reduce.3.cloned.1.call-update) | async-done | bytes 524304
  75.1 2.2 %dynamic-slice_bitcast_fusion = bf16[4,1,1,4,4096]{4,3,2,1,0:T(4,128)(2,1)} fusion(bf16[4,1,4,4,4096]{4,3,2,0,1:T(4,128)(2,1)} %all-reduce.3.cloned.1.call-done, u32[]{:T(128)} %bitcast.38), kind=kLoop, calls=%fused_computation.18 | loop fusion | bytes 262148 | tf_op jit(solution)/shard_map/reduce_scatter | solution.py:41
  77.3 4.6 %all-to-all-start.1 = ((bf16[4,1,1,4,4096]{4,3,2,1,0:T(4,128)(2,1)}), bf16[4,1,1,4,4096]{4,3,2,1,0:T(4,128)(2,1)S(1)}, u32[]{:S(2)}, u32[]{:S(2)}) async-start(bf16[4,1,1,4,4096]{4,3,2,1,0:T(4,128)(2,1)} %dynamic-slice_bitcast_fusion), calls=%async_computation.1 | async-start | bytes 262144 | tf_op jit(solution)/shard_map/all_to_all | solution.py:44
  81.9 0.1 compare_select_fusion
  82.0 5.8 %all-to-all-done.1 = bf16[4,1,1,4,4096]{4,3,2,1,0:T(4,128)(2,1)S(1)} async-done(((bf16[4,1,1,4,4096]{4,3,2,1,0:T(4,128)(2,1)}), bf16[4,1,1,4,4096]{4,3,2,1,0:T(4,128)(2,1)S(1)}, u32[]{:S(2)}, u32[]{:S(2)}) %all-to-all-start.1) | async-done | bytes 131104 | tf_op jit(solution)/shard_map/all_to_all | solution.py:44
  87.9 0.6 gather_fusion
  88.5 0.1 reshape.171
  88.6 0.9 multiply_reduce_fusion
  (7 shorter events, 0.1 us)
Async XLA Ops:
  6.5 34.3 %copy-start = (bf16[1,384,4096]{2,1,0:T(8,128)(2,1)S(1)}, bf16[1,384,4096]{2,1,0:T(8,128)(2,1)}, u32[]{:S(2)}) copy-start(bf16[1,384,4096]{2,1,0:T(8,128)(2,1)} %param.11) | copy-start | bytes 9437188
  6.5 68.6 %all-reduce.3.cloned.1.call-start = ((), (), s32[]{:S(2)}) async-start(), calls=%async_computation.2 | async-start | bytes 1048576
  36.4 3.3 %copy-start.2 = (bf16[1,384,4096]{2,1,0:T(8,128)(2,1)S(1)}, bf16[1,384,4096]{2,1,0:T(8,128)(2,1)}, u32[]{:S(2)}) copy-start(bf16[1,384,4096]{2,1,0:T(8,128)(2,1)} %param.10) | copy-start | bytes 9437188
  40.9 1.7 %copy-start.1 = (f32[4,2]{0,1:T(2,128)S(1)}, f32[4,2]{0,1:T(2,128)}, u32[]{:S(2)}) copy-start(f32[4,2]{0,1:T(2,128)} %param.8) | copy-start | bytes 100
  40.9 1.8 %copy-start.3 = (u32[32]{0:T(128)S(1)}, u32[32]{0:T(128)}, u32[]{:S(2)}) copy-start(u32[32]{0:T(128)} %constant.62) | copy-start | bytes 388
  77.3 10.5 %all-to-all-start.1 = ((bf16[4,1,1,4,4096]{4,3,2,1,0:T(4,128)(2,1)}), bf16[4,1,1,4,4096]{4,3,2,1,0:T(4,128)(2,1)S(1)}, u32[]{:S(2)}, u32[]{:S(2)}) async-start(bf16[4,1,1,4,4096]{4,3,2,1,0:T(4,128)(2,1)} %dynamic-slice_bitcast_fusion), calls=%async_computation.1 | async-start | bytes 262144 | tf_op jit(solution)/shard_map/all_to_all | solution.py:44
Sparse Core Ops, SparseCore 0:
  42.5 32.5 all-reduce.2
where the time goes:
time: 96.7 us; the launch traced here: 96.3 us
  waiting for transfers between devices  37.6 us (39%)
  blocking collectives  20.8 us (22%)
  between operations  13.5 us (14%)
  local copies, waits for them, and re-layouts  11.2 us (12%)
  matrix products  5.98 us (6%)
  starting transfers between devices  4.6 us (5%)
  other arithmetic  2.56 us (3%)
    unnamed x2, waiting for transfers between devices  31.8 us
    all_to_all x1, blocking collectives, on_device(): lax.all_to_all(send, 'expert', split_axis=0, concat_axis=0, tiled=True)  20.8 us
    all_to_all x1, waiting for transfers between devices, on_device(): lax.all_to_all(summed, 'expert', split_axis=0, concat_axis=0, tiled=True)  5.83 us
    all_to_all x1, starting transfers between devices, on_device(): lax.all_to_all(summed, 'expert', split_axis=0, concat_axis=0, tiled=True)  4.6 us
    dot_general x1, matrix products, on_device(): jnp.einsum('sepcd,efd->sepcf', received, w_gate, preferred_element_type=j...  3.25 us
    reduce_scatter x1, local copies, waits for them, and re-layouts, on_device(): lax.psum_scatter(partial_out.astype(jnp.bfloat16), 'etp', scatter_dimensi...  2.25 us
    scatter x1, local copies, waits for them, and re-layouts, on_device(): jnp.zeros((experts * n_etp * capsub, width), jnp.bfloat16).at[dest]  2.19 us
    reshape x1, local copies, waits for them, and re-layouts, on_device(): send = send.reshape(n_expert, exp_dev, n_etp, capsub, width)  2.05 us
  transfers between devices with their start and end apart: 2, of which 2 were waited for; matrix products, arithmetic and copies ran while one was open for 1% of the time, Pallas kernels for 0%

commit v1 on v0

v1 whole, which is shorter than its diff:
```python
import functools

import jax
import jax.numpy as jnp
from jax import lax
from jax.experimental import pallas as pl
from jax.experimental.pallas import tpu as pltpu
from jax.sharding import PartitionSpec as P

MESH = pl.DeviceIdType.MESH
BF16 = jnp.bfloat16
F32 = jnp.float32


def layer_kernel(
    n_exp, n_etp, n_chunk,
    tok_ref, ids_ref, rw_ref, wg_ref, wu_ref, wd_ref, out_ref,
    xbuf, wgb, wub, wdb, pbuf, recva, sendb, recvb, ownb, sendc, recvc,
    wsem, dsem, tsem, zs, zr, xs, xr, cs, cr, as_, ar, bs, br, es, er,
):
    n_x = n_etp // 2
    rows = tok_ref.shape[0]
    own_rows = rows // n_etp
    width = tok_ref.shape[1]
    kq = width // n_etp
    cw = width // n_chunk
    grp = n_exp * own_rows
    e = lax.axis_index("expert")
    q = lax.axis_index("etp")
    x = q // 2
    c = q % 2

    def etp_of(co, xo):
        return lax.rem(x + xo, n_x) * 2 + lax.rem(c + co, 2)

    slots = [(co, xo) for xo in range(n_x) for co in range(2)]

    def quarter(co, xo):
        return pl.ds(pl.multiple_of(etp_of(co, xo) * kq, kq), kq)

    tok_copies, w_copies, d_copies = {}, {}, []
    for co, xo in slots:
        i = co * n_x + xo
        t = pltpu.make_async_copy(tok_ref.at[:, quarter(co, xo)], xbuf.at[i, e], tsem.at[i])
        t.start()
        tok_copies[i] = t
    for co, xo in slots:
        i = co * n_x + xo
        a = pltpu.make_async_copy(wg_ref.at[0, :, quarter(co, xo)], wgb.at[i], wsem.at[i, 0])
        b = pltpu.make_async_copy(wu_ref.at[0, :, quarter(co, xo)], wub.at[i], wsem.at[i, 1])
        a.start()
        b.start()
        w_copies[i] = (a, b)
    for j in range(n_chunk):
        d = pltpu.make_async_copy(wd_ref.at[0, :, pl.ds(j * cw, cw)], wdb.at[j], dsem.at[j])
        d.start()
        d_copies.append(d)

    barrier = pltpu.get_barrier_semaphore()
    partners = [{"etp": etp_of(1, 0)}]
    partners += [{"etp": etp_of(0, xo)} for xo in range(1, n_x)]
    partners += [{"expert": lax.rem(e + k, n_exp)} for k in range(1, n_exp)]
    for dev in partners:
        pl.semaphore_signal(barrier, inc=1, device_id=dev, device_id_type=MESH)
    pl.semaphore_wait(barrier, len(partners))

    pending = []
    z_copies = []
    for k in range(1, n_exp):
        cp = pltpu.make_async_remote_copy(
            tok_ref.at[:, quarter(0, 0)], xbuf.at[0, e], zs.at[k - 1], zr.at[k - 1],
            device_id={"expert": lax.rem(e + k, n_exp)}, device_id_type=MESH)
        cp.start()
        z_copies.append(cp)
        pending.append(cp)

    x_copies, c_copies = {}, {}

    def to_core(xo, k):
        blk = lax.rem(e + n_exp - k, n_exp)
        cp = pltpu.make_async_remote_copy(
            xbuf.at[xo, blk], xbuf.at[n_x + xo, blk], cs.at[xo, k - 1], cr.at[xo, k - 1],
            device_id={"etp": etp_of(1, 0)}, device_id_type=MESH)
        cp.start()
        c_copies[xo, k] = cp
        pending.append(cp)

    for k in range(1, n_exp):
        blk = lax.rem(e + n_exp - k, n_exp)
        z_copies[k - 1].wait_recv()
        for xo in range(1, n_x):
            cp = pltpu.make_async_remote_copy(
                xbuf.at[0, blk], xbuf.at[n_x - xo, blk], xs.at[xo - 1, k - 1], xr.at[xo - 1, k - 1],
                device_id={"etp": etp_of(0, xo)}, device_id_type=MESH)
            cp.start()
            x_copies[xo, k] = cp
            pending.append(cp)
        to_core(0, k)

    def partial_dots(i):
        tok_copies[i].wait()
        w_copies[i][0].wait()
        w_copies[i][1].wait()
        xv = xbuf[i].reshape(n_exp * rows, kq)
        dims = (((1,), (1,)), ((), ()))
        return (lax.dot_general(xv, wgb[i], dims, preferred_element_type=F32),
                lax.dot_general(xv, wub[i], dims, preferred_element_type=F32))

    gate, upper = partial_dots(0)
    for xo in range(1, n_x):
        for k in range(1, n_exp):
            x_copies[xo, k].wait_recv()
            to_core(n_x - xo, k)
    for co, xo in slots[1:]:
        if co == 1:
            for k in range(1, n_exp):
                c_copies[xo, k].wait_recv()
        g, u = partial_dots(co * n_x + xo)
        gate += g
        upper += u
    hidden = (gate / (1.0 + jnp.exp(-gate)) * upper).astype(BF16)

    total = n_exp * rows
    m = lax.broadcasted_iota(jnp.int32, (total, total), 0)
    n = lax.broadcasted_iota(jnp.int32, (total, total), 1)
    slot = m // grp
    dest = lax.rem(x + slot % n_x, n_x) * 2 + lax.rem(c + slot // n_x, 2)
    source = (m % grp) // own_rows * rows + dest * own_rows + m % own_rows
    perm = (n == source).astype(F32).astype(BF16)
    hidden = jnp.dot(perm, hidden, preferred_element_type=F32).astype(BF16)

    half = n_x * grp
    a_copies, b_copies, e_copies = [], {}, {}
    for j in range(n_chunk):
        d_copies[j].wait()
        pbuf[j] = jnp.dot(hidden, wdb[j], preferred_element_type=F32).astype(BF16)
        cp = pltpu.make_async_remote_copy(
            pbuf.at[j, pl.ds(half, half)], recva.at[j], as_.at[j], ar.at[j],
            device_id={"etp": etp_of(1, 0)}, device_id_type=MESH)
        cp.start()
        a_copies.append(cp)
        pending.append(cp)

    for j in range(n_chunk):
        a_copies[j].wait_recv()
        for xo in range(1, n_x):
            at = pl.ds(xo * grp, grp)
            sendb[j, xo - 1] = (pbuf[j, at].astype(F32) + recva[j, at].astype(F32)).astype(BF16)
            cp = pltpu.make_async_remote_copy(
                sendb.at[j, xo - 1], recvb.at[j, xo - 1], bs.at[j, xo - 1], br.at[j, xo - 1],
                device_id={"etp": etp_of(0, xo)}, device_id_type=MESH)
            cp.start()
            b_copies[j, xo] = cp
            pending.append(cp)
        at = pl.ds(0, grp)
        ownb[j] = pbuf[j, at].astype(F32) + recva[j, at].astype(F32)

    for j in range(n_chunk):
        total_j = ownb[j]
        for xo in range(1, n_x):
            b_copies[j, xo].wait_recv()
            total_j += recvb[j, xo - 1].astype(F32)
        total_j = total_j.astype(BF16)
        for z in range(n_exp):
            sendc[j, z] = total_j[z * own_rows:(z + 1) * own_rows]
        for k in range(1, n_exp):
            to = lax.rem(e + k, n_exp)
            cp = pltpu.make_async_remote_copy(
                sendc.at[j, to], recvc.at[j, k], es.at[j, k - 1], er.at[j, k - 1],
                device_id={"expert": to}, device_id_type=MESH)
            cp.start()
            e_copies[j, k] = cp
            pending.append(cp)

    ids = ids_ref[pl.ds(0, own_rows), :]
    for t in range(1, n_etp):
        ids = jnp.where(q == t, ids_ref[pl.ds(t * own_rows, own_rows), :], ids)
    rw = rw_ref[...]
    combine = rw / jnp.sum(rw, axis=1, keepdims=True)
    weights = []
    for k in range(n_exp):
        src = lax.rem(e + n_exp - k, n_exp)
        weights.append(jnp.sum(jnp.where(ids == src, combine, 0.0), axis=1, keepdims=True))

    for j in range(n_chunk):
        mixed = sendc[j, e].astype(F32) * weights[0]
        for k in range(1, n_exp):
            e_copies[j, k].wait_recv()
            mixed += recvc[j, k].astype(F32) * weights[k]
        out_ref[:, pl.ds(j * cw, cw)] = mixed.astype(BF16)

    for cp in pending:
        cp.wait_send()


def on_device(tokens, expert_ids, route_weights, w_gate, w_up, w_down):
    n_exp = lax.axis_size("expert")
    n_etp = lax.axis_size("etp")
    rows, width = tokens.shape
    own_rows = rows // n_etp
    exp_dev, ff, _ = w_gate.shape
    assert exp_dev == 1 and n_etp % 2 == 0
    n_x = n_etp // 2
    n_chunk = 4
    kq, cw, grp = width // n_etp, width // n_chunk, n_exp * own_rows
    half = n_x * grp
    dma = pltpu.SemaphoreType.DMA
    vmem = pl.BlockSpec(memory_space=pltpu.VMEM)
    hbm = pl.BlockSpec(memory_space=pl.ANY)
    return pl.pallas_call(
        functools.partial(layer_kernel, n_exp, n_etp, n_chunk),
        out_shape=jax.ShapeDtypeStruct((own_rows, width), BF16),
        in_specs=[hbm, vmem, vmem, hbm, hbm, hbm],
        out_specs=vmem,
        scratch_shapes=[
            pltpu.VMEM((n_etp, n_exp, rows, kq), BF16),
            pltpu.VMEM((n_etp, ff, kq), BF16),
            pltpu.VMEM((n_etp, ff, kq), BF16),
            pltpu.VMEM((n_chunk, ff, cw), BF16),
            pltpu.VMEM((n_chunk, 2 * half, cw), BF16),
            pltpu.VMEM((n_chunk, half, cw), BF16),
            pltpu.VMEM((n_chunk, n_x - 1, grp, cw), BF16),
            pltpu.VMEM((n_chunk, n_x - 1, grp, cw), BF16),
            pltpu.VMEM((n_chunk, grp, cw), F32),
            pltpu.VMEM((n_chunk, n_exp, own_rows, cw), BF16),
            pltpu.VMEM((n_chunk, n_exp, own_rows, cw), BF16),
            dma((n_etp, 2)),
            dma((n_chunk,)),
            dma((n_etp,)),
            dma((n_exp - 1,)), dma((n_exp - 1,)),
            dma((n_x - 1, n_exp - 1)), dma((n_x - 1, n_exp - 1)),
            dma((n_x, n_exp - 1)), dma((n_x, n_exp - 1)),
            dma((n_chunk,)), dma((n_chunk,)),
            dma((n_chunk, n_x - 1)), dma((n_chunk, n_x - 1)),
            dma((n_chunk, n_exp - 1)), dma((n_chunk, n_exp - 1)),
        ],
        compiler_params=pltpu.CompilerParams(collective_id=0, has_side_effects=True),
    )(tokens, expert_ids, route_weights, w_gate, w_up, w_down)


def solution(mesh):
    in_specs = (
        P(("group", "expert"), None),
        P(("group", "expert"), None),
        P(("group", "expert", "etp"), None),
        P("expert", "etp", None),
        P("expert", "etp", None),
        P("expert", "etp", None),
    )
    out_specs = P(("group", "expert", "etp"), None)
    return jax.shard_map(
        on_device, mesh=mesh, in_specs=in_specs, out_specs=out_specs, check_vma=False
    )
```

time: 96.7 us -> 31.6 us (0.33)
  waiting for transfers between devices: 37.6 us -> 0 us
  Pallas kernels: 0 us -> 27.3 us
  blocking collectives: 20.8 us -> 0 us
  between operations: 13.5 us -> 0.01 us
  local copies, waits for them, and re-layouts: 11.2 us -> 4.06 us
  matrix products: 5.98 us -> 0 us
  starting transfers between devices: 4.6 us -> 0 us
  other arithmetic: 2.56 us -> 0 us
    unnamed x2 -> x0, waiting for transfers between devices: 31.8 us -> none
    pallas_call x0 -> x1, Pallas kernels: none -> 27.3 us  [on_device(): pl.pallas_call(functools.partial(layer_kernel, n_exp, n_etp, n_chunk), ou...]
    all_to_all x1 -> x0, blocking collectives: 20.8 us -> none  [on_device(): lax.all_to_all(send, 'expert', split_axis=0, concat_axis=0, tiled=True)]
    dot_general x3 -> x0, matrix products: 5.98 us -> none  [the longest x1 3.25 us: on_device(): jnp.einsum('sepcd,efd->sepcf', received, w_gate, preferred_element_type=j...]
    all_to_all x1 -> x0, waiting for transfers between devices: 5.83 us -> none  [on_device(): lax.all_to_all(summed, 'expert', split_axis=0, concat_axis=0, tiled=True)]
    all_to_all x1 -> x0, starting transfers between devices: 4.6 us -> none  [on_device(): lax.all_to_all(summed, 'expert', split_axis=0, concat_axis=0, tiled=True)]
    reshape x6 -> x0, local copies, waits for them, and re-layouts: 3.14 us -> none  [the longest x1 2.05 us: on_device(): send = send.reshape(n_expert, exp_dev, n_etp, capsub, width)]
    unnamed x10 -> x3, local copies, waits for them, and re-layouts: 1.49 us -> 4.06 us
  transfers between devices with their start and end apart: 2 -> 0, of which waited for: 2 -> 0; matrix products, arithmetic and copies ran while one was open for 1% -> 0% of each run, Pallas kernels for 0% -> 0%
where the time goes in v1:
time: 31.6 us; the launch traced here: 31.3 us
  Pallas kernels  27.3 us (86%)
  local copies, waits for them, and re-layouts  4.06 us (13%)
    pallas_call x1, Pallas kernels, on_device(): pl.pallas_call(functools.partial(layer_kernel, n_exp, n_etp, n_chunk), ou...  27.3 us
    unnamed x3, local copies, waits for them, and re-layouts  4.06 us

profile of v1, /device:TPU:0, one launch (start us, length us, event | category | flops | bytes accessed | tf_op | source)
XLA Modules:
  0.0 31.3 jit_solution(13330266879826480098)
XLA Ops:
  0.0 1.3 %copy.8.rw_ref = f32[4,2]{1,0:T(4,128)} copy(f32[4,2]{0,1:T(2,128)} %param.8) | data formatting | bytes 64 | tf_op args[2]
  1.3 1.4 %copy.7.ids_ref = s32[16,2]{1,0:T(8,128)} copy(s32[16,2]{0,1:T(2,128)} %param.7) | data formatting | bytes 256 | tf_op args[1]
  2.7 27.3 %shard_map.64 = bf16[4,4096]{1,0:T(4,128)(2,1)} custom-call(bf16[16,4096]{1,0:T(8,128)(2,1)} %tok_ref.1, s32[16,2]{1,0:T(8,128)} %copy.7.ids_ref, f32[4,2]{1,0:T(4,128)} %copy.8.rw_ref, bf16[1,384,4096]{2,1,0:T(8,128)(2,1)} %wg_ref.1, bf16[1,384,4096]{2,1,0:T(8,128)(2,1)} %wu_ref.1, bf16[1,384,4096]{2,1,0:T(8,128)(2,1)} %wd_ref.1), custom_call_target="tpu_custom_call" | custom-call | tf_op jit(solution)/shard_map/pallas_call | solution.py:210
  30.0 1.4 %copy.10 = bf16[4,4096]{1,0:T(4,128)(2,1)} copy(bf16[4,4096]{1,0:T(4,128)(2,1)} %shard_map.64) | data formatting | bytes 65536

commit v2 on v1

--- a/solution.py
+++ b/solution.py
@@ -16,7 +16,7 @@
     n_exp, n_etp, n_chunk,
     tok_ref, ids_ref, rw_ref, wg_ref, wu_ref, wd_ref, out_ref,
     xbuf, wgb, wub, wdb, pbuf, recva, sendb, recvb, ownb, sendc, recvc,
-    wsem, dsem, tsem, zs, zr, xs, xr, cs, cr, as_, ar, bs, br, es, er,
+    idsb, rwb, ssem, wsem, dsem, tsem, zs, zr, xs, xr, cs, cr, as_, ar, bs, br, es, er,
 ):
     n_x = n_etp // 2
     rows = tok_ref.shape[0]
@@ -32,6 +32,17 @@
 
     def etp_of(co, xo):
         return lax.rem(x + xo, n_x) * 2 + lax.rem(c + co, 2)
+
+    high = e // (n_exp // 2)
+
+    def farthest(k):
+        down, up = n_exp - 1 - k, k
+        down = down - (e - down + n_exp) // n_exp
+        up = up + (up - e + n_exp) // n_exp
+        return (1 - high) * down + high * up
+
+    far = [farthest(k) for k in range(n_exp - 1)]
+    near = far[::-1]
 
     slots = [(co, xo) for xo in range(n_x) for co in range(2)]
 
@@ -56,6 +67,10 @@
         d.start()
         d_copies.append(d)
 
+    small_copies = [pltpu.make_async_copy(ids_ref, idsb, ssem.at[0]),
+                    pltpu.make_async_copy(rw_ref, rwb, ssem.at[1])]
+    for cp in small_copies:
+        cp.start()
     barrier = pltpu.get_barrier_semaphore()
     partners = [{"etp": etp_of(1, 0)}]
     partners += [{"etp": etp_of(0, xo)} for xo in range(1, n_x)]
@@ -65,19 +80,22 @@
     pl.semaphore_wait(barrier, len(partners))
 
     pending = []
-    z_copies = []
-    for k in range(1, n_exp):
+    for to in far:
         cp = pltpu.make_async_remote_copy(
-            tok_ref.at[:, quarter(0, 0)], xbuf.at[0, e], zs.at[k - 1], zr.at[k - 1],
-            device_id={"expert": lax.rem(e + k, n_exp)}, device_id_type=MESH)
-        cp.start()
-        z_copies.append(cp)
+            tok_ref.at[:, quarter(0, 0)], xbuf.at[0, e], zs.at[to], zr.at[e],
+            device_id={"expert": to}, device_id_type=MESH)
+        cp.start()
         pending.append(cp)
 
+    def z_arrival(src):
+        return pltpu.make_async_remote_copy(
+            tok_ref.at[:, quarter(0, 0)], xbuf.at[0, src], zs.at[src], zr.at[src],
+            device_id={"expert": src}, device_id_type=MESH)
+
     x_copies, c_copies = {}, {}
 
     def to_core(xo, k):
-        blk = lax.rem(e + n_exp - k, n_exp)
+        blk = near[k - 1]
         cp = pltpu.make_async_remote_copy(
             xbuf.at[xo, blk], xbuf.at[n_x + xo, blk], cs.at[xo, k - 1], cr.at[xo, k - 1],
             device_id={"etp": etp_of(1, 0)}, device_id_type=MESH)
@@ -86,8 +104,8 @@
         pending.append(cp)
 
     for k in range(1, n_exp):
-        blk = lax.rem(e + n_exp - k, n_exp)
-        z_copies[k - 1].wait_recv()
+        blk = near[k - 1]
+        z_arrival(blk).wait_recv()
         for xo in range(1, n_x):
             cp = pltpu.make_async_remote_copy(
                 xbuf.at[0, blk], xbuf.at[n_x - xo, blk], xs.at[xo - 1, k - 1], xr.at[xo - 1, k - 1],
@@ -130,7 +148,7 @@
     hidden = jnp.dot(perm, hidden, preferred_element_type=F32).astype(BF16)
 
     half = n_x * grp
-    a_copies, b_copies, e_copies = [], {}, {}
+    a_copies, b_copies = [], {}
     for j in range(n_chunk):
         d_copies[j].wait()
         pbuf[j] = jnp.dot(hidden, wdb[j], preferred_element_type=F32).astype(BF16)
@@ -163,30 +181,37 @@
         total_j = total_j.astype(BF16)
         for z in range(n_exp):
             sendc[j, z] = total_j[z * own_rows:(z + 1) * own_rows]
-        for k in range(1, n_exp):
-            to = lax.rem(e + k, n_exp)
+        for to in far:
             cp = pltpu.make_async_remote_copy(
-                sendc.at[j, to], recvc.at[j, k], es.at[j, k - 1], er.at[j, k - 1],
+                sendc.at[j, to], recvc.at[j, e], es.at[j, to], er.at[j, e],
                 device_id={"expert": to}, device_id_type=MESH)
             cp.start()
-            e_copies[j, k] = cp
             pending.append(cp)
 
-    ids = ids_ref[pl.ds(0, own_rows), :]
-    for t in range(1, n_etp):
-        ids = jnp.where(q == t, ids_ref[pl.ds(t * own_rows, own_rows), :], ids)
-    rw = rw_ref[...]
-    combine = rw / jnp.sum(rw, axis=1, keepdims=True)
+    for cp in small_copies:
+        cp.wait()
+    top = idsb.shape[0]
+
+    def column(row, first):
+        lanes = lax.broadcasted_iota(jnp.int32, (own_rows, row.shape[1]), 1)
+        here = lax.broadcasted_iota(jnp.int32, (own_rows, row.shape[1]), 0) + first
+        return jnp.sum(jnp.where(lanes == here, row, jnp.zeros_like(row)), axis=1, keepdims=True)
+
+    rws = rwb[...]
+    combine = rws / jnp.sum(rws, axis=0, keepdims=True)
+    chosen = [column(idsb[k:k + 1, :], q * own_rows) for k in range(top)]
+    share = [column(combine[k:k + 1, :], 0) for k in range(top)]
     weights = []
-    for k in range(n_exp):
-        src = lax.rem(e + n_exp - k, n_exp)
-        weights.append(jnp.sum(jnp.where(ids == src, combine, 0.0), axis=1, keepdims=True))
+    for src in [e] + near:
+        weights.append(sum(jnp.where(i == src, w, 0.0) for i, w in zip(chosen, share)))
 
     for j in range(n_chunk):
         mixed = sendc[j, e].astype(F32) * weights[0]
-        for k in range(1, n_exp):
-            e_copies[j, k].wait_recv()
-            mixed += recvc[j, k].astype(F32) * weights[k]
+        for k, src in enumerate(near):
+            pltpu.make_async_remote_copy(
+                sendc.at[j, src], recvc.at[j, src], es.at[j, src], er.at[j, src],
+                device_id={"expert": src}, device_id_type=MESH).wait_recv()
+            mixed += recvc[j, src].astype(F32) * weights[k + 1]
         out_ref[:, pl.ds(j * cw, cw)] = mixed.astype(BF16)
 
     for cp in pending:
@@ -209,8 +234,8 @@
     hbm = pl.BlockSpec(memory_space=pl.ANY)
     return pl.pallas_call(
         functools.partial(layer_kernel, n_exp, n_etp, n_chunk),
-        out_shape=jax.ShapeDtypeStruct((own_rows, width), BF16),
-        in_specs=[hbm, vmem, vmem, hbm, hbm, hbm],
+        out_shape=pltpu.VMEM((own_rows, width), BF16),
+        in_specs=[hbm] * 6,
         out_specs=vmem,
         scratch_shapes=[
             pltpu.VMEM((n_etp, n_exp, rows, kq), BF16),
@@ -224,18 +249,21 @@
             pltpu.VMEM((n_chunk, grp, cw), F32),
             pltpu.VMEM((n_chunk, n_exp, own_rows, cw), BF16),
             pltpu.VMEM((n_chunk, n_exp, own_rows, cw), BF16),
+            pltpu.VMEM(expert_ids.shape[::-1], jnp.int32),
+            pltpu.VMEM(route_weights.shape[::-1], F32),
+            dma((2,)),
             dma((n_etp, 2)),
             dma((n_chunk,)),
             dma((n_etp,)),
-            dma((n_exp - 1,)), dma((n_exp - 1,)),
+            dma((n_exp,)), dma((n_exp,)),
             dma((n_x - 1, n_exp - 1)), dma((n_x - 1, n_exp - 1)),
             dma((n_x, n_exp - 1)), dma((n_x, n_exp - 1)),
             dma((n_chunk,)), dma((n_chunk,)),
             dma((n_chunk, n_x - 1)), dma((n_chunk, n_x - 1)),
-            dma((n_chunk, n_exp - 1)), dma((n_chunk, n_exp - 1)),
+            dma((n_chunk, n_exp)), dma((n_chunk, n_exp)),
         ],
         compiler_params=pltpu.CompilerParams(collective_id=0, has_side_effects=True),
-    )(tokens, expert_ids, route_weights, w_gate, w_up, w_down)
+    )(tokens, expert_ids.T, route_weights.T, w_gate, w_up, w_down)
 
 
 def solution(mesh):

time: 31.6 us -> 25.8 us (0.82)
  local copies, waits for them, and re-layouts: 4.06 us -> 0.62 us
  Pallas kernels: 27.3 us -> 25 us
    unnamed x3 -> x1, local copies, waits for them, and re-layouts: 4.06 us -> 0.62 us
    pallas_call x1, Pallas kernels: 27.3 us -> 25 us  [on_device(): pl.pallas_call(functools.partial(layer_kernel, n_exp, n_etp, n_chunk), ou...]
where the time goes in v2:
time: 25.8 us; the launch traced here: 25.7 us
  Pallas kernels  25 us (97%)
  local copies, waits for them, and re-layouts  0.62 us (2%)
    pallas_call x1, Pallas kernels, on_device(): pl.pallas_call(functools.partial(layer_kernel, n_exp, n_etp, n_chunk), ou...  25 us
    unnamed x1, local copies, waits for them, and re-layouts  0.62 us

profile of v2, /device:TPU:0, one launch (start us, length us, event | category | flops | bytes accessed | tf_op | source)
XLA Modules:
  0.0 25.7 jit_solution(10749634085980036849)
XLA Ops:
  0.0 25.0 %shard_map.64 = bf16[4,4096]{1,0:T(4,128)(2,1)S(1)} custom-call(bf16[16,4096]{1,0:T(8,128)(2,1)} %tok_ref.1, s32[2,16]{1,0:T(2,128)} %bitcast.2, f32[2,4]{1,0:T(2,128)} %bitcast.3, bf16[1,384,4096]{2,1,0:T(8,128)(2,1)} %wg_ref.1, bf16[1,384,4096]{2,1,0:T(8,128)(2,1)} %wu_ref.1, bf16[1,384,4096]{2,1,0:T(8,128)(2,1)} %wd_ref.1), custom_call_target="tpu_custom_call" | custom-call | tf_op jit(solution)/shard_map/pallas_call | solution.py:235
  25.1 0.6 %copy.8 = bf16[4,4096]{1,0:T(4,128)(2,1)} copy(bf16[4,4096]{1,0:T(4,128)(2,1)S(1)} %shard_map.64) | data formatting | bytes 65536

commit v3 on v2

--- a/solution.py
+++ b/solution.py
@@ -15,8 +15,8 @@
 def layer_kernel(
     n_exp, n_etp, n_chunk,
     tok_ref, ids_ref, rw_ref, wg_ref, wu_ref, wd_ref, out_ref,
-    xbuf, wgb, wub, wdb, pbuf, recva, sendb, recvb, ownb, sendc, recvc,
-    idsb, rwb, ssem, wsem, dsem, tsem, zs, zr, xs, xr, cs, cr, as_, ar, bs, br, es, er,
+    xbuf, wb, wdb, pbuf, recva, sendb, recvb, ownb, sendc, recvc,
+    acc, idsb, rwb, ssem, wsem, dsem, tsem, zs, zr, xs, xr, cs, cr, as_, ar, bs, br, es, er,
 ):
     n_x = n_etp // 2
     rows = tok_ref.shape[0]
@@ -44,12 +44,16 @@
     far = [farthest(k) for k in range(n_exp - 1)]
     near = far[::-1]
 
+    def several(ref, sent, arrived):
+        return pltpu.make_async_remote_copy(
+            ref, ref, sent, arrived, device_id={"etp": etp_of(1, 0)}, device_id_type=MESH)
+
     slots = [(co, xo) for xo in range(n_x) for co in range(2)]
 
     def quarter(co, xo):
         return pl.ds(pl.multiple_of(etp_of(co, xo) * kq, kq), kq)
 
-    tok_copies, w_copies, d_copies = {}, {}, []
+    tok_copies, d_copies = {}, []
     for co, xo in slots:
         i = co * n_x + xo
         t = pltpu.make_async_copy(tok_ref.at[:, quarter(co, xo)], xbuf.at[i, e], tsem.at[i])
@@ -57,11 +61,8 @@
         tok_copies[i] = t
     for co, xo in slots:
         i = co * n_x + xo
-        a = pltpu.make_async_copy(wg_ref.at[0, :, quarter(co, xo)], wgb.at[i], wsem.at[i, 0])
-        b = pltpu.make_async_copy(wu_ref.at[0, :, quarter(co, xo)], wub.at[i], wsem.at[i, 1])
-        a.start()
-        b.start()
-        w_copies[i] = (a, b)
+        for h, w_ref in enumerate((wg_ref, wu_ref)):
+            pltpu.make_async_copy(w_ref.at[0, :, quarter(co, xo)], wb.at[i, h], wsem.at[i]).start()
     for j in range(n_chunk):
         d = pltpu.make_async_copy(wd_ref.at[0, :, pl.ds(j * cw, cw)], wdb.at[j], dsem.at[j])
         d.start()
@@ -79,63 +80,66 @@
         pl.semaphore_signal(barrier, inc=1, device_id=dev, device_id_type=MESH)
     pl.semaphore_wait(barrier, len(partners))
 
-    pending = []
     for to in far:
         cp = pltpu.make_async_remote_copy(
-            tok_ref.at[:, quarter(0, 0)], xbuf.at[0, e], zs.at[to], zr.at[e],
+            tok_ref.at[:, quarter(0, 0)], xbuf.at[0, e], zs, zr.at[e],
             device_id={"expert": to}, device_id_type=MESH)
         cp.start()
-        pending.append(cp)
 
     def z_arrival(src):
         return pltpu.make_async_remote_copy(
-            tok_ref.at[:, quarter(0, 0)], xbuf.at[0, src], zs.at[src], zr.at[src],
+            tok_ref.at[:, quarter(0, 0)], xbuf.at[0, src], zs, zr.at[src],
             device_id={"expert": src}, device_id_type=MESH)
 
-    x_copies, c_copies = {}, {}
+    x_copies = {}
 
     def to_core(xo, k):
         blk = near[k - 1]
         cp = pltpu.make_async_remote_copy(
-            xbuf.at[xo, blk], xbuf.at[n_x + xo, blk], cs.at[xo, k - 1], cr.at[xo, k - 1],
+            xbuf.at[xo, blk], xbuf.at[n_x + xo, blk], cs, cr.at[xo],
             device_id={"etp": etp_of(1, 0)}, device_id_type=MESH)
         cp.start()
-        c_copies[xo, k] = cp
-        pending.append(cp)
 
     for k in range(1, n_exp):
         blk = near[k - 1]
         z_arrival(blk).wait_recv()
         for xo in range(1, n_x):
             cp = pltpu.make_async_remote_copy(
-                xbuf.at[0, blk], xbuf.at[n_x - xo, blk], xs.at[xo - 1, k - 1], xr.at[xo - 1, k - 1],
+                xbuf.at[0, blk], xbuf.at[n_x - xo, blk], xs, xr.at[xo - 1, k - 1],
                 device_id={"etp": etp_of(0, xo)}, device_id_type=MESH)
             cp.start()
             x_copies[xo, k] = cp
-            pending.append(cp)
         to_core(0, k)
 
-    def partial_dots(i):
+    def add_slot(co, xo):
+        i = co * n_x + xo
         tok_copies[i].wait()
-        w_copies[i][0].wait()
-        w_copies[i][1].wait()
+        pltpu.make_async_copy(wb.at[i], wb.at[i], wsem.at[i]).wait()
         xv = xbuf[i].reshape(n_exp * rows, kq)
         dims = (((1,), (1,)), ((), ()))
-        return (lax.dot_general(xv, wgb[i], dims, preferred_element_type=F32),
-                lax.dot_general(xv, wub[i], dims, preferred_element_type=F32))
-
-    gate, upper = partial_dots(0)
+        for h in range(2):
+            part = lax.dot_general(xv, wb[i, h], dims, preferred_element_type=F32)
+            if i == 0:
+                acc[h] = part
+            else:
+                acc[h] += part
+
+    def from_core(xo):
+        several(xbuf.at[n_x + xo, pl.ds(0, n_exp - 1)], cs, cr.at[xo]).wait_recv()
+
+    add_slot(0, 0)
+    from_core(0)
+    add_slot(1, 0)
     for xo in range(1, n_x):
         for k in range(1, n_exp):
             x_copies[xo, k].wait_recv()
             to_core(n_x - xo, k)
-    for co, xo in slots[1:]:
-        if co == 1:
-            for k in range(1, n_exp):
-                c_copies[xo, k].wait_recv()
-        g, u = partial_dots(co * n_x + xo)
-        gate += g
-        upper += u
+    for xo in range(1, n_x):
+        add_slot(0, xo)
+    for xo in range(1, n_x):
+        from_core(xo)
+        add_slot(1, xo)
+    gate, upper = acc[0], acc[1]
     hidden = (gate / (1.0 + jnp.exp(-gate)) * upper).astype(BF16)
 
     total = n_exp * rows
@@ -153,11 +157,10 @@
         d_copies[j].wait()
         pbuf[j] = jnp.dot(hidden, wdb[j], preferred_element_type=F32).astype(BF16)
         cp = pltpu.make_async_remote_copy(
-            pbuf.at[j, pl.ds(half, half)], recva.at[j], as_.at[j], ar.at[j],
+            pbuf.at[j, pl.ds(half, half)], recva.at[j], as_, ar.at[j],
             device_id={"etp": etp_of(1, 0)}, device_id_type=MESH)
         cp.start()
         a_copies.append(cp)
-        pending.append(cp)
 
     for j in range(n_chunk):
         a_copies[j].wait_recv()
@@ -165,11 +168,10 @@
             at = pl.ds(xo * grp, grp)
             sendb[j, xo - 1] = (pbuf[j, at].astype(F32) + recva[j, at].astype(F32)).astype(BF16)
             cp = pltpu.make_async_remote_copy(
-                sendb.at[j, xo - 1], recvb.at[j, xo - 1], bs.at[j, xo - 1], br.at[j, xo - 1],
+                sendb.at[j, xo - 1], recvb.at[j, xo - 1], bs, br.at[j, xo - 1],
                 device_id={"etp": etp_of(0, xo)}, device_id_type=MESH)
             cp.start()
             b_copies[j, xo] = cp
-            pending.append(cp)
         at = pl.ds(0, grp)
         ownb[j] = pbuf[j, at].astype(F32) + recva[j, at].astype(F32)
 
@@ -183,10 +185,9 @@
             sendc[j, z] = total_j[z * own_rows:(z + 1) * own_rows]
         for to in far:
             cp = pltpu.make_async_remote_copy(
-                sendc.at[j, to], recvc.at[j, e], es.at[j, to], er.at[j, e],
+                sendc.at[j, to], recvc.at[j, e], es, er.at[j],
                 device_id={"expert": to}, device_id_type=MESH)
             cp.start()
-            pending.append(cp)
 
     for cp in small_copies:
         cp.wait()
@@ -207,15 +208,18 @@
 
     for j in range(n_chunk):
         mixed = sendc[j, e].astype(F32) * weights[0]
+        several(recvc.at[j, pl.ds(0, n_exp - 1)], es, er.at[j]).wait_recv()
         for k, src in enumerate(near):
-            pltpu.make_async_remote_copy(
-                sendc.at[j, src], recvc.at[j, src], es.at[j, src], er.at[j, src],
-                device_id={"expert": src}, device_id_type=MESH).wait_recv()
             mixed += recvc[j, src].astype(F32) * weights[k + 1]
         out_ref[:, pl.ds(j * cw, cw)] = mixed.astype(BF16)
 
-    for cp in pending:
-        cp.wait_send()
+    remote = n_exp - 1
+    several(xbuf.at[0, pl.ds(0, remote)], zs, zr.at[0]).wait_send()
+    several(xbuf.at[pl.ds(0, n_x - 1), pl.ds(0, remote)], xs, xr.at[0, 0]).wait_send()
+    several(xbuf.at[pl.ds(0, n_x), pl.ds(0, remote)], cs, cr.at[0]).wait_send()
+    several(recva, as_, ar.at[0]).wait_send()
+    several(sendb, bs, br.at[0, 0]).wait_send()
+    several(sendc.at[:, pl.ds(0, remote)], es, er.at[0]).wait_send()
 
 
 def on_device(tokens, expert_ids, route_weights, w_gate, w_up, w_down):
@@ -239,8 +243,7 @@
         out_specs=vmem,
         scratch_shapes=[
             pltpu.VMEM((n_etp, n_exp, rows, kq), BF16),
-            pltpu.VMEM((n_etp, ff, kq), BF16),
-            pltpu.VMEM((n_etp, ff, kq), BF16),
+            pltpu.VMEM((n_etp, 2, ff, kq), BF16),
             pltpu.VMEM((n_chunk, ff, cw), BF16),
             pltpu.VMEM((n_chunk, 2 * half, cw), BF16),
             pltpu.VMEM((n_chunk, half, cw), BF16),
@@ -249,18 +252,19 @@
             pltpu.VMEM((n_chunk, grp, cw), F32),
             pltpu.VMEM((n_chunk, n_exp, own_rows, cw), BF16),
             pltpu.VMEM((n_chunk, n_exp, own_rows, cw), BF16),
+            pltpu.VMEM((2, n_exp * rows, ff), F32),
             pltpu.VMEM(expert_ids.shape[::-1], jnp.int32),
             pltpu.VMEM(route_weights.shape[::-1], F32),
             dma((2,)),
-            dma((n_etp, 2)),
+            dma((n_etp,)),
             dma((n_chunk,)),
             dma((n_etp,)),
-            dma((n_exp,)), dma((n_exp,)),
-            dma((n_x - 1, n_exp - 1)), dma((n_x - 1, n_exp - 1)),
-            dma((n_x, n_exp - 1)), dma((n_x, n_exp - 1)),
-            dma((n_chunk,)), dma((n_chunk,)),
-            dma((n_chunk, n_x - 1)), dma((n_chunk, n_x - 1)),
-            dma((n_chunk, n_exp)), dma((n_chunk, n_exp)),
+            dma, dma((n_exp,)),
+            dma, dma((n_x - 1, n_exp - 1)),
+            dma, dma((n_x,)),
+            dma, dma((n_chunk,)),
+            dma, dma((n_chunk, n_x - 1)),
+            dma, dma((n_chunk,)),
         ],
         compiler_params=pltpu.CompilerParams(collective_id=0, has_side_effects=True),
     )(tokens, expert_ids.T, route_weights.T, w_gate, w_up, w_down)

time: 25.8 us -> 24.6 us (0.953)
  Pallas kernels: 25 us -> 23.8 us
    pallas_call x1, Pallas kernels: 25 us -> 23.8 us  [on_device(): pl.pallas_call(functools.partial(layer_kernel, n_exp, n_etp, n_chunk), ou...]
where the time goes in v3:
time: 24.6 us; the launch traced here: 24.4 us
  Pallas kernels  23.8 us (97%)
  local copies, waits for them, and re-layouts  0.62 us (3%)
    pallas_call x1, Pallas kernels, on_device(): pl.pallas_call(functools.partial(layer_kernel, n_exp, n_etp, n_chunk), ou...  23.8 us
    unnamed x1, local copies, waits for them, and re-layouts  0.62 us

profile of v3, /device:TPU:0, one launch (start us, length us, event | category | flops | bytes accessed | tf_op | source)
XLA Modules:
  0.0 24.4 jit_solution(9753456253009329980)
XLA Ops:
  0.0 23.8 %shard_map.64 = bf16[4,4096]{1,0:T(4,128)(2,1)S(1)} custom-call(bf16[16,4096]{1,0:T(8,128)(2,1)} %tok_ref.1, s32[2,16]{1,0:T(2,128)} %bitcast.2, f32[2,4]{1,0:T(2,128)} %bitcast.3, bf16[1,384,4096]{2,1,0:T(8,128)(2,1)} %wg_ref.1, bf16[1,384,4096]{2,1,0:T(8,128)(2,1)} %wu_ref.1, bf16[1,384,4096]{2,1,0:T(8,128)(2,1)} %wd_ref.1), custom_call_target="tpu_custom_call" | custom-call | tf_op jit(solution)/shard_map/pallas_call | solution.py:239
  23.8 0.6 %copy.8 = bf16[4,4096]{1,0:T(4,128)(2,1)} copy(bf16[4,4096]{1,0:T(4,128)(2,1)S(1)} %shard_map.64) | data formatting | bytes 65536
